TPU v7x, 32 devices: a whole 2x2x4 slice. The times are simulated.
32 devices in a mesh: groups: 2 (over x), ctx: 16 (over z, y, core).
Axes of the slice: x: 2, y: 2, z: 4, core: 2. Of those that a mesh axis runs over, the one named last changes fastest.
Arguments:
- queries: bfloat16 [16384, 4096], P(('groups', 'ctx')), parts along dimension 0, may hold values from -50 to 50
- keys: bfloat16 [16384, 512], P(('groups', 'ctx')), parts along dimension 0, may hold values from -6 to 6
- values: bfloat16 [16384, 512], P(('groups', 'ctx')), parts along dimension 0, may hold values from -6 to 6
- doc_lengths: int32 [16], P('groups'), parts along dimension 0, may hold values from 1 to 2048, 8192 in all
Outputs:
- attended: bfloat16 [16384, 4096], P(('groups', 'ctx')), parts along dimension 0
There are 2 independent parts, one for each index of `groups`. A program takes and returns all parts, laid end to end along the dimension named above; each array names one. Nothing has to cross between parts.
Inputs may be any that keep to these rules, and one draw needn't show every extreme that they name: `doc_lengths`: lengths sum to 8192; the longest is exactly 2048.
All inputs are finite; a program needn't handle non-finite values.
Results may differ from a plain program's by a relative error of at most 0.0038.
Values may be sent and summed in bfloat16 or wider, within the bound.
A program may use at most 320 MiB of HBM per device.

v0:
```python
import functools
import math

import jax
import jax.numpy as jnp
from jax import lax
from jax.experimental import pallas as pl
from jax.experimental.pallas import tpu as pltpu
from jax.sharding import PartitionSpec as P

QUERY_HEADS = 32
KEY_VALUE_HEADS = 4
HEAD_SIZE = 128
SPAN_DEV = 4
GROUP = QUERY_HEADS // KEY_VALUE_HEADS
TILE = 256
NEGATIVE = -1e30
SCALE = HEAD_SIZE ** (-0.5) * math.log2(math.e)


def from_behind(value, axis, steps):
    count = lax.axis_size(axis)
    initial, last = (max(0, -steps), min(count, count - steps))
    return lax.ppermute(value, axis, [(source, source + steps) for source in range(initial, last)])


def attend_tile(first_row, heads, query_of, store, row_bounds, kt, vx, scores, weights, reach):
    window = reach + TILE
    steps = window // TILE
    rows = lax.broadcasted_iota(jnp.int32, (TILE, HEAD_SIZE), 0) + first_row
    one_hot = ((rows >= row_bounds[0:1, :]) & (rows < row_bounds[1:2, :])).astype(jnp.float32)
    one_hot = one_hot.astype(jnp.bfloat16)
    causal = lax.broadcasted_iota(jnp.int32, (TILE, TILE), 1) <= lax.broadcasted_iota(
        jnp.int32, (TILE, TILE), 0
    )
    causal = jnp.concatenate([causal, causal], axis=0)
    tags = jnp.concatenate([one_hot, one_hot], axis=0)

    def pair(head, slot):
        both = jnp.concatenate([query_of(head), query_of(head + 1)], axis=0)
        left = jnp.concatenate([both, tags], axis=1)
        peak = None
        for step in range(steps):
            columns = pl.ds(pl.multiple_of(first_row + step * TILE, TILE), TILE)
            part = jnp.dot(left, kt[:, columns], preferred_element_type=jnp.float32)
            if step == steps - 1:
                part = jnp.where(causal, part, NEGATIVE)
            scores[slot, :, step * TILE : (step + 1) * TILE] = part
            high = jnp.maximum(part[:, :HEAD_SIZE], part[:, HEAD_SIZE:])
            peak = high if peak is None else jnp.maximum(peak, high)
        top = jnp.max(peak, axis=1, keepdims=True) * SCALE
        for step in range(steps):
            columns = slice(step * TILE, (step + 1) * TILE)
            weights[slot, :, columns] = jnp.exp2(scores[slot, :, columns] * SCALE - top).astype(
                jnp.bfloat16
            )
        keys_at = pl.ds(pl.multiple_of(first_row, TILE), window)
        total = jnp.dot(weights[slot], vx[keys_at, :], preferred_element_type=jnp.float32)
        result = (total[:, :HEAD_SIZE] / total[:, HEAD_SIZE:]).astype(jnp.bfloat16)
        store(head, result[:TILE])
        store(head + 1, result[TILE:])

    @pl.loop(0, heads // 4)
    def _(quad):
        for slot in range(2):
            pair(quad * 4 + slot * 2, slot)


def kernel(reach, *refs):
    blocks = SPAN_DEV + 1
    row_bounds, column_bounds, q = refs[:3]
    ks = refs[3 : 3 + blocks]
    vs = refs[3 + blocks : 3 + 2 * blocks]
    out, kt, vx, scores, weights = refs[3 + 2 * blocks :]
    group, tile = pl.program_id(0), pl.program_id(1)
    depth = ks[0].shape[0]

    @pl.when((group == 0) & (tile == 0))
    def _():
        place = lax.broadcasted_iota(jnp.int32, (HEAD_SIZE, TILE), 1) - reach
        for part in range(kt.shape[1] // TILE):
            at = place + part * TILE
            inside = (at >= column_bounds[:, 0:1]) & (at < column_bounds[:, 1:2])
            kt[HEAD_SIZE:, part * TILE : (part + 1) * TILE] = jnp.where(
                inside, 0.0, NEGATIVE
            ).astype(jnp.bfloat16)
        vx[:, HEAD_SIZE:] = jnp.ones((vx.shape[0], HEAD_SIZE), jnp.bfloat16)

    @pl.when(tile == 0)
    def _():
        for block in range(blocks):
            span = slice(block * depth, (block + 1) * depth)
            kt[:HEAD_SIZE, span] = ks[block][...].T
            vx[span, :HEAD_SIZE] = vs[block][...]

    def query_of(head):
        return q[:, pl.ds(pl.multiple_of(head * HEAD_SIZE, HEAD_SIZE), HEAD_SIZE)]

    def store(head, value):
        out[:, pl.ds(pl.multiple_of(head * HEAD_SIZE, HEAD_SIZE), HEAD_SIZE)] = value

    attend_tile(tile * TILE, GROUP, query_of, store, row_bounds, kt, vx, scores, weights, reach)


def body(queries, keys, values, doc_lengths):
    row_total = queries.shape[0]
    reach = SPAN_DEV * row_total
    start = lax.axis_index("ctx") * row_total
    docs = doc_lengths.shape[0]
    index = jnp.arange(HEAD_SIZE)
    lengths = jnp.zeros((HEAD_SIZE,), jnp.int32).at[:docs].set(doc_lengths)
    ends = jnp.sum(jnp.where(index[None, :] <= index[:, None], lengths[None, :], 0), axis=1)
    high = ends - start
    low = high - lengths
    row_bounds = jnp.concatenate([low[None], high[None], jnp.zeros((6, HEAD_SIZE), jnp.int32)])
    column_bounds = jnp.stack([low, high], axis=1)

    rows = jnp.concatenate([keys, values], axis=1)
    parts = [from_behind(rows, "ctx", distance) for distance in range(SPAN_DEV, 0, -1)] + [rows]
    wide = GROUP * HEAD_SIZE
    key_specs = [pl.BlockSpec((row_total, HEAD_SIZE), lambda g, t: (0, g)) for _ in parts]
    value_specs = [
        pl.BlockSpec((row_total, HEAD_SIZE), lambda g, t: (0, g + KEY_VALUE_HEADS)) for _ in parts
    ]
    whole = reach + row_total
    return pl.pallas_call(
        functools.partial(kernel, reach),
        grid=(KEY_VALUE_HEADS, row_total // TILE),
        out_shape=jax.ShapeDtypeStruct(queries.shape, jnp.bfloat16),
        in_specs=[
            pl.BlockSpec((8, HEAD_SIZE), lambda g, t: (0, 0)),
            pl.BlockSpec((HEAD_SIZE, 2), lambda g, t: (0, 0)),
            pl.BlockSpec((TILE, wide), lambda g, t: (t, g)),
        ]
        + key_specs
        + value_specs,
        out_specs=pl.BlockSpec((TILE, wide), lambda g, t: (t, g)),
        scratch_shapes=[
            pltpu.VMEM((2 * HEAD_SIZE, whole), jnp.bfloat16),
            pltpu.VMEM((whole, 2 * HEAD_SIZE), jnp.bfloat16),
            pltpu.VMEM((2, 2 * TILE, reach + TILE), jnp.float32),
            pltpu.VMEM((2, 2 * TILE, reach + TILE), jnp.bfloat16),
        ],
        compiler_params=pltpu.CompilerParams(vmem_limit_bytes=48 * 1024 * 1024),
    )(row_bounds, column_bounds, queries, *parts, *parts)


def solution(mesh):
    placed = (
        P(("groups", "ctx"), None),
        P(("groups", "ctx"), None),
        P(("groups", "ctx"), None),
        P("groups"),
    )
    return jax.shard_map(
        body, mesh=mesh, in_specs=placed, out_specs=P(("groups", "ctx"), None), check_vma=False
    )
```

profile of v0, /device:TPU:13, one launch (start us, length us, event | category | flops | bytes accessed | tf_op | source)
XLA Modules:
  0.0 158.9 jit_solution(10152524930576682329)
XLA Ops:
  0.0 1.1 constant_dynamic-update-slice_fusion.1
  1.1 1.1 constant_dynamic-update-slice_fusion.refs_7_.refs_12_
  2.2 3.7 %collective-permute-start.3 = (bf16[512,1024]{1,0:T(8,128)(2,1)S(1)}, bf16[512,1024]{1,0:T(8,128)(2,1)S(1)}, u32[]{:S(2)}, u32[]{:S(2)}) collective-permute-start(bf16[512,1024]{1,0:T(8,128)(2,1)S(1)} %constant_dynamic-update-slice_fusion.refs_7_.refs_12_), channel_id=1, source_target_pairs={{0,1},{1,2},{2,3},{3,4},{4,5},{5,6},{6,7},{7,8},{8,9},{9,10},{10,1... | collective-permute-start | bytes 3145736 | tf_op jit(solution)/shard_map/ppermute | solution.py:24
  5.9 3.1 %collective-permute-start.2 = (bf16[512,1024]{1,0:T(8,128)(2,1)S(1)}, bf16[512,1024]{1,0:T(8,128)(2,1)S(1)}, u32[]{:S(2)}, u32[]{:S(2)}) collective-permute-start(bf16[512,1024]{1,0:T(8,128)(2,1)S(1)} %constant_dynamic-update-slice_fusion.refs_7_.refs_12_), channel_id=1, source_target_pairs={{0,2},{1,3},{2,4},{3,5},{4,6},{5,7},{6,8},{7,9},{8,10},{9,11},{10,... | collective-permute-start | bytes 3145736 | tf_op jit(solution)/shard_map/ppermute | solution.py:24
  9.1 2.3 %collective-permute-start.1 = (bf16[512,1024]{1,0:T(8,128)(2,1)S(1)}, bf16[512,1024]{1,0:T(8,128)(2,1)}, u32[]{:S(2)}, u32[]{:S(2)}) collective-permute-start(bf16[512,1024]{1,0:T(8,128)(2,1)S(1)} %constant_dynamic-update-slice_fusion.refs_7_.refs_12_), channel_id=1, source_target_pairs={{0,3},{1,4},{2,5},{3,6},{4,7},{5,8},{6,9},{7,10},{8,11},{9,12},{10... | collective-permute-start | bytes 3145736 | tf_op jit(solution)/shard_map/ppermute | solution.py:24
  11.4 2.9 %collective-permute-start = (bf16[512,1024]{1,0:T(8,128)(2,1)S(1)}, bf16[512,1024]{1,0:T(8,128)(2,1)}, u32[]{:S(2)}, u32[]{:S(2)}) collective-permute-start(bf16[512,1024]{1,0:T(8,128)(2,1)S(1)} %constant_dynamic-update-slice_fusion.refs_7_.refs_12_), channel_id=1, source_target_pairs={{0,4},{1,5},{2,6},{3,7},{4,8},{5,9},{6,10},{7,11},{8,12},{9,13},{1... | collective-permute-start | bytes 3145736 | tf_op jit(solution)/shard_map/ppermute | solution.py:24
  14.2 0.7 scatter.4
  14.9 0.1 pad.7.clone
  15.0 0.1 select_reduce_fusion
  15.1 0.7 subtract_bitcast_fusion
  15.8 0.1 copy.8.refs_1_
  15.9 0.7 subtract_bitcast_fusion.1
  16.6 0.1 add_add_fusion.refs_0_
  16.6 9.8 %collective-permute-done.3.refs_6_.refs_11_ = bf16[512,1024]{1,0:T(8,128)(2,1)S(1)} collective-permute-done((bf16[512,1024]{1,0:T(8,128)(2,1)S(1)}, bf16[512,1024]{1,0:T(8,128)(2,1)S(1)}, u32[]{:S(2)}, u32[]{:S(2)}) %collective-permute-start.3) | collective-permute-done | bytes 1048608 | tf_op jit(solution)/shard_map/ppermute | solution.py:24
  26.4 23.5 %collective-permute-done.2.refs_5_.refs_10_ = bf16[512,1024]{1,0:T(8,128)(2,1)S(1)} collective-permute-done((bf16[512,1024]{1,0:T(8,128)(2,1)S(1)}, bf16[512,1024]{1,0:T(8,128)(2,1)S(1)}, u32[]{:S(2)}, u32[]{:S(2)}) %collective-permute-start.2) | collective-permute-done | bytes 1048608 | tf_op jit(solution)/shard_map/ppermute | solution.py:24
  49.9 21.4 %collective-permute-done.1.refs_4_.refs_9_ = bf16[512,1024]{1,0:T(8,128)(2,1)} collective-permute-done((bf16[512,1024]{1,0:T(8,128)(2,1)S(1)}, bf16[512,1024]{1,0:T(8,128)(2,1)}, u32[]{:S(2)}, u32[]{:S(2)}) %collective-permute-start.1) | collective-permute-done | bytes 1048608 | tf_op jit(solution)/shard_map/ppermute | solution.py:24
  71.3 14.5 %collective-permute-done.refs_3_.refs_8_ = bf16[512,1024]{1,0:T(8,128)(2,1)} collective-permute-done((bf16[512,1024]{1,0:T(8,128)(2,1)S(1)}, bf16[512,1024]{1,0:T(8,128)(2,1)}, u32[]{:S(2)}, u32[]{:S(2)}) %collective-permute-start) | collective-permute-done | bytes 1048608 | tf_op jit(solution)/shard_map/ppermute | solution.py:24
  85.8 73.1 %shard_map.46 = bf16[512,4096]{1,0:T(8,128)(2,1)} custom-call(s32[8,128]{1,0:T(8,128)S(1)} %add_add_fusion.refs_0_, s32[128,2]{1,0:T(8,128)S(1)} %copy.8.refs_1_, bf16[512,4096]{1,0:T(8,128)(2,1)} %refs_2_.1, bf16[512,1024]{1,0:T(8,128)(2,1)} %collective-permute-done.refs_3_.refs_8_, bf16[512,1024]{1,0:T(8,128)(2,1)} %collective-permute-done.1.refs_4_.refs_9_, ...), custom_call_target="tpu_custom_call" | custom-call | tf_op jit(solution)/shard_map/pallas_call | solution.py:126
  (2 shorter events, 0.0 us)
Async XLA Ops:
  2.2 24.2 %collective-permute-start.3 = (bf16[512,1024]{1,0:T(8,128)(2,1)S(1)}, bf16[512,1024]{1,0:T(8,128)(2,1)S(1)}, u32[]{:S(2)}, u32[]{:S(2)}) collective-permute-start(bf16[512,1024]{1,0:T(8,128)(2,1)S(1)} %constant_dynamic-update-slice_fusion.refs_7_.refs_12_), channel_id=1, source_target_pairs={{0,1},{1,2},{2,3},{3,4},{4,5},{5,6},{6,7},{7,8},{8,9},{9,10},{10,1... | collective-permute-start | bytes 3145736 | tf_op jit(solution)/shard_map/ppermute | solution.py:24
  5.9 44.0 %collective-permute-start.2 = (bf16[512,1024]{1,0:T(8,128)(2,1)S(1)}, bf16[512,1024]{1,0:T(8,128)(2,1)S(1)}, u32[]{:S(2)}, u32[]{:S(2)}) collective-permute-start(bf16[512,1024]{1,0:T(8,128)(2,1)S(1)} %constant_dynamic-update-slice_fusion.refs_7_.refs_12_), channel_id=1, source_target_pairs={{0,2},{1,3},{2,4},{3,5},{4,6},{5,7},{6,8},{7,9},{8,10},{9,11},{10,... | collective-permute-start | bytes 3145736 | tf_op jit(solution)/shard_map/ppermute | solution.py:24
  9.1 62.2 %collective-permute-start.1 = (bf16[512,1024]{1,0:T(8,128)(2,1)S(1)}, bf16[512,1024]{1,0:T(8,128)(2,1)}, u32[]{:S(2)}, u32[]{:S(2)}) collective-permute-start(bf16[512,1024]{1,0:T(8,128)(2,1)S(1)} %constant_dynamic-update-slice_fusion.refs_7_.refs_12_), channel_id=1, source_target_pairs={{0,3},{1,4},{2,5},{3,6},{4,7},{5,8},{6,9},{7,10},{8,11},{9,12},{10... | collective-permute-start | bytes 3145736 | tf_op jit(solution)/shard_map/ppermute | solution.py:24
  11.4 74.4 %collective-permute-start = (bf16[512,1024]{1,0:T(8,128)(2,1)S(1)}, bf16[512,1024]{1,0:T(8,128)(2,1)}, u32[]{:S(2)}, u32[]{:S(2)}) collective-permute-start(bf16[512,1024]{1,0:T(8,128)(2,1)S(1)} %constant_dynamic-update-slice_fusion.refs_7_.refs_12_), channel_id=1, source_target_pairs={{0,4},{1,5},{2,6},{3,7},{4,8},{5,9},{6,10},{7,11},{8,12},{9,13},{1... | collective-permute-start | bytes 3145736 | tf_op jit(solution)/shard_map/ppermute | solution.py:24
where the time goes:
time: 159 us
  Pallas kernels  73.1 us (46%)
  waiting for transfers between devices  69.2 us (44%)
  starting transfers between devices  12 us (8%)
  local copies, waits for them, and re-layouts  3.07 us (2%)
    pallas_call x1, Pallas kernels, body(): pl.pallas_call(functools.partial(kernel, reach), grid=(KEY_VALUE_HEADS, r...  73.1 us
    ppermute x4, waiting for transfers between devices, from_behind(): lax.ppermute(value, axis, [(source, source + steps) for source in range(i...  69.2 us
    ppermute x4, starting transfers between devices, from_behind(): lax.ppermute(value, axis, [(source, source + steps) for source in range(i...  12 us
  transfers between devices with their start and end apart: 4, of which 4 were waited for; matrix products, arithmetic and copies ran while one was open for 1% of the time, Pallas kernels for 0%

commit v1 on v0

v1 whole, which is shorter than its diff:
```python
import functools
import math

import jax
import jax.numpy as jnp
from jax import lax
from jax.experimental import pallas as pl
from jax.experimental.pallas import tpu as pltpu
from jax.sharding import PartitionSpec as P

QUERY_HEADS = 32
KEY_VALUE_HEADS = 4
HEAD_SIZE = 128
SPAN_DEV = 4
GROUP = QUERY_HEADS // KEY_VALUE_HEADS
TILE = 256
NEGATIVE = -1e30
SCALE = HEAD_SIZE ** (-0.5) * math.log2(math.e)


def attend_tile(first_row, heads, query_of, store, row_bounds, kt, vx, scores, weights, reach):
    window = reach + TILE
    steps = window // TILE
    rows = lax.broadcasted_iota(jnp.int32, (TILE, HEAD_SIZE), 0) + first_row
    one_hot = ((rows >= row_bounds[0:1, :]) & (rows < row_bounds[1:2, :])).astype(jnp.float32)
    one_hot = one_hot.astype(jnp.bfloat16)
    causal = lax.broadcasted_iota(jnp.int32, (TILE, TILE), 1) <= lax.broadcasted_iota(
        jnp.int32, (TILE, TILE), 0
    )
    causal = jnp.concatenate([causal, causal], axis=0)
    tags = jnp.concatenate([one_hot, one_hot], axis=0)

    def scored(left, slot, step):
        columns = pl.ds(pl.multiple_of(first_row + step * TILE, TILE), TILE)
        part = jnp.dot(left, kt[:, columns], preferred_element_type=jnp.float32)
        if step == steps - 1:
            part = jnp.where(causal, part, NEGATIVE)
        scores[slot, :, step * TILE : (step + 1) * TILE] = part
        return jnp.maximum(part[:, :HEAD_SIZE], part[:, HEAD_SIZE:])

    def weighed(slot, step, top):
        columns = slice(step * TILE, (step + 1) * TILE)
        weights[slot, :, columns] = jnp.exp2(scores[slot, :, columns] * SCALE - top).astype(
            jnp.bfloat16
        )

    def left_of(pair):
        both = jnp.concatenate([query_of(2 * pair), query_of(2 * pair + 1)], axis=0)
        return jnp.concatenate([both, tags], axis=1)

    top = None
    pairs = heads // 2
    for pair in range(pairs + 1):
        slot, last = pair % 2, (pair + 1) % 2
        left = left_of(pair) if pair < pairs else None
        peak = None
        for step in range(steps):
            if pair < pairs:
                high = scored(left, slot, step)
                peak = high if peak is None else jnp.maximum(peak, high)
            if pair > 0:
                weighed(last, step, top)
        if pair < pairs:
            top = jnp.max(peak, axis=1, keepdims=True) * SCALE
        if pair > 0:
            keys_at = pl.ds(pl.multiple_of(first_row, TILE), window)
            total = jnp.dot(weights[last], vx[keys_at, :], preferred_element_type=jnp.float32)
            result = (total[:, :HEAD_SIZE] / total[:, HEAD_SIZE:]).astype(jnp.bfloat16)
            store(2 * pair - 2, result[:TILE])
            store(2 * pair - 1, result[TILE:])


def transfers(keys, values, land, send_sem, recv_sem):
    count = lax.axis_size("ctx")
    me = lax.axis_index("ctx")
    core, odd = me % 2, (me // 2) % 2
    ahead, behind = (me + SPAN_DEV) % count, (me + count - SPAN_DEV) % count
    across = me + 2 - 4 * odd
    partner = me + 1 - 2 * core
    own = (keys, values)

    def copy(source, slot, head, kind, target):
        return pltpu.make_async_remote_copy(
            src_ref=source,
            dst_ref=land.at[slot, kind, head],
            send_sem=send_sem.at[slot, kind, head],
            recv_sem=recv_sem.at[slot, kind, head],
            device_id={"ctx": target},
            device_id_type=pl.DeviceIdType.MESH,
        )

    def mine(head, kind):
        return own[kind].at[:, head * HEAD_SIZE : (head + 1) * HEAD_SIZE]

    def both(action):
        for kind in range(2):
            action(kind)

    def begin():
        barrier = pltpu.get_barrier_semaphore()
        for other in (ahead, behind, across, partner):
            pl.semaphore_signal(
                barrier, inc=1, device_id={"ctx": other}, device_id_type=pl.DeviceIdType.MESH
            )
        pl.semaphore_wait(barrier, 4)
        for head in range(KEY_VALUE_HEADS):
            both(lambda kind: copy(mine(head, kind), 3, head, kind, ahead).start())

            @pl.when(odd == 0)
            def _():
                both(lambda kind: copy(mine(head, kind), 1, head, kind, across).start())

            @pl.when(core == 0)
            def _():
                both(lambda kind: copy(mine(head, kind), 0, head, kind, partner).start())

    def far(head):
        both(lambda kind: copy(mine(head, kind), 3, head, kind, ahead).wait_recv())

        @pl.when(odd == 1)
        def _():
            both(lambda kind: copy(land.at[3, kind, head], 1, head, kind, across).start())

        @pl.when(core == 1)
        def _():
            both(lambda kind: copy(land.at[3, kind, head], 2, head, kind, partner).start())

    def near(head):
        both(lambda kind: copy(mine(head, kind), 1, head, kind, across).wait_recv())

        @pl.when(core == 0)
        def _():
            both(lambda kind: copy(land.at[1, kind, head], 2, head, kind, partner).start())

        @pl.when(core == 1)
        def _():
            both(lambda kind: copy(land.at[1, kind, head], 0, head, kind, partner).start())

    def beside(head):
        for slot in (0, 2):
            both(lambda kind: copy(mine(head, kind), slot, head, kind, partner).wait_recv())

    def finish():
        for head in range(KEY_VALUE_HEADS):
            for slot in range(SPAN_DEV):
                both(lambda kind: copy(mine(head, kind), slot, head, kind, ahead).wait_send())

    return begin, far, near, beside, finish


def kernel(lengths, keys, values, q, out, row_bounds, land, kt, vx, scores, weights, send_sem, recv_sem):
    group, tile = pl.program_id(0), pl.program_id(1)
    groups, tiles = KEY_VALUE_HEADS, q_tiles(keys)
    depth = keys.shape[0]
    reach = SPAN_DEV * depth
    begin, far, near, beside, finish = transfers(keys, values, land, send_sem, recv_sem)

    @pl.when((group == 0) & (tile == 0))
    def _():
        begin()
        lane = lax.broadcasted_iota(jnp.int32, (8, HEAD_SIZE), 1)
        line = lax.broadcasted_iota(jnp.int32, (HEAD_SIZE, TILE), 0)
        row_low = row_high = jnp.zeros((8, HEAD_SIZE), jnp.int32)
        low = high = jnp.zeros((HEAD_SIZE, TILE), jnp.int32)
        first = -lax.axis_index("ctx") * depth
        for doc in range(lengths.shape[0]):
            last = first + lengths[doc]
            row_low, row_high = jnp.where(lane == doc, first, row_low), jnp.where(lane == doc, last, row_high)
            low, high = jnp.where(line == doc, first, low), jnp.where(line == doc, last, high)
            first = last
        row_bounds[0], row_bounds[1] = row_low, row_high
        place = lax.broadcasted_iota(jnp.int32, (HEAD_SIZE, TILE), 1) - reach
        for part in range(kt.shape[1] // TILE):
            at = place + part * TILE
            kt[HEAD_SIZE:, part * TILE : (part + 1) * TILE] = jnp.where(
                (at >= low) & (at < high), 0.0, NEGATIVE
            ).astype(jnp.bfloat16)
        vx[:, HEAD_SIZE:] = jnp.ones((vx.shape[0], HEAD_SIZE), jnp.bfloat16)

    for head in range(groups):

        @pl.when((group == head) & (tile == 0))
        def _():
            if head == 0:
                far(0)
                near(0)
                far(1)
            beside(head)
            span = slice(reach, reach + depth)
            columns = slice(head * HEAD_SIZE, (head + 1) * HEAD_SIZE)
            kt[:HEAD_SIZE, span] = keys[:, columns].T
            vx[span, :HEAD_SIZE] = values[:, columns]

        if head + 1 < groups:

            @pl.when((group == head) & (tile == tiles - 1))
            def _():
                near(head + 1)
                if head + 2 < groups:
                    far(head + 2)

    @pl.when(tile == 0)
    def _():
        for slot in range(SPAN_DEV):
            span = slice(reach - (slot + 1) * depth, reach - slot * depth)
            kt[:HEAD_SIZE, span] = land[slot, 0, group].T
            vx[span, :HEAD_SIZE] = land[slot, 1, group]

    def query_of(head):
        return q[:, head * HEAD_SIZE : (head + 1) * HEAD_SIZE]

    def store(head, value):
        out[:, head * HEAD_SIZE : (head + 1) * HEAD_SIZE] = value

    bounds = jnp.concatenate([row_bounds[0][:1], row_bounds[1][:1]], axis=0)
    attend_tile(tile * TILE, GROUP, query_of, store, bounds, kt, vx, scores, weights, reach)

    @pl.when((group == groups - 1) & (tile == tiles - 1))
    def _():
        finish()


def q_tiles(keys):
    return keys.shape[0] // TILE


def body(queries, keys, values, doc_lengths):
    row_total = queries.shape[0]
    reach = SPAN_DEV * row_total
    wide = GROUP * HEAD_SIZE
    whole = reach + row_total
    travel = (SPAN_DEV, 2, KEY_VALUE_HEADS)
    return pl.pallas_call(
        kernel,
        grid=(KEY_VALUE_HEADS, row_total // TILE),
        out_shape=jax.ShapeDtypeStruct(queries.shape, jnp.bfloat16),
        in_specs=[
            pl.BlockSpec(memory_space=pltpu.SMEM),
            pl.BlockSpec(memory_space=pltpu.VMEM),
            pl.BlockSpec(memory_space=pltpu.VMEM),
            pl.BlockSpec((TILE, wide), lambda g, t: (t, g)),
        ],
        out_specs=pl.BlockSpec((TILE, wide), lambda g, t: (t, g)),
        scratch_shapes=[
            pltpu.VMEM((2, 8, HEAD_SIZE), jnp.int32),
            pltpu.VMEM(travel + (row_total, HEAD_SIZE), jnp.bfloat16),
            pltpu.VMEM((2 * HEAD_SIZE, whole), jnp.bfloat16),
            pltpu.VMEM((whole, 2 * HEAD_SIZE), jnp.bfloat16),
            pltpu.VMEM((2, 2 * TILE, reach + TILE), jnp.float32),
            pltpu.VMEM((2, 2 * TILE, reach + TILE), jnp.bfloat16),
            pltpu.SemaphoreType.DMA(travel),
            pltpu.SemaphoreType.DMA(travel),
        ],
        compiler_params=pltpu.CompilerParams(
            vmem_limit_bytes=48 * 1024 * 1024, collective_id=0, has_side_effects=True
        ),
    )(doc_lengths, keys, values, queries)


def solution(mesh):
    placed = (
        P(("groups", "ctx"), None),
        P(("groups", "ctx"), None),
        P(("groups", "ctx"), None),
        P("groups"),
    )
    return jax.shard_map(
        body, mesh=mesh, in_specs=placed, out_specs=P(("groups", "ctx"), None), check_vma=False
    )
```

time: 159 us -> 79.5 us (0.50)
  the two profiles are of different devices: /device:TPU:13 before, /device:TPU:0 now
where the time goes in v1:
time: 79.5 us; the launch traced here: 78.3 us
  Pallas kernels  73.5 us (92%)
  local copies, waits for them, and re-layouts  4.75 us (6%)
    pallas_call x1, Pallas kernels, body(): pl.pallas_call(kernel, grid=(KEY_VALUE_HEADS, row_total // TILE), out_sha...  73.5 us
    unnamed x7, local copies, waits for them, and re-layouts  4.75 us

profile of v1, /device:TPU:0, one launch (start us, length us, event | category | flops | bytes accessed | tf_op | source)
XLA Modules:
  0.0 78.3 jit_solution(3121401761682899258)
XLA Ops:
  0.0 0.0 copy-start
  0.0 1.0 %copy-done = bf16[512,512]{1,0:T(8,128)(2,1)S(1)} copy-done((bf16[512,512]{1,0:T(8,128)(2,1)S(1)}, bf16[512,512]{1,0:T(8,128)(2,1)}, u32[]{:S(2)}) %copy-start) | copy-done | bytes 524312
  1.0 0.0 copy-start.1
  1.0 1.0 %copy-done.1 = bf16[512,512]{1,0:T(8,128)(2,1)S(1)} copy-done((bf16[512,512]{1,0:T(8,128)(2,1)S(1)}, bf16[512,512]{1,0:T(8,128)(2,1)}, u32[]{:S(2)}) %copy-start.1) | copy-done | bytes 524312
  2.1 0.0 copy-start.2
  2.1 0.7 copy-done.2
  2.7 73.5 %shard_map.46 = bf16[512,4096]{1,0:T(8,128)(2,1)S(1)} custom-call(s32[8]{0:T(128)S(1)} %copy-done.2, bf16[512,512]{1,0:T(8,128)(2,1)S(1)} %copy-done, bf16[512,512]{1,0:T(8,128)(2,1)S(1)} %copy-done.1, bf16[512,4096]{1,0:T(8,128)(2,1)} %q.1), custom_call_target="tpu_custom_call" | custom-call | tf_op jit(solution)/shard_map/pallas_call | solution.py:233
  76.2 2.0 %copy.6 = bf16[512,4096]{1,0:T(8,128)(2,1)} copy(bf16[512,4096]{1,0:T(8,128)(2,1)S(1)} %shard_map.46) | data formatting | bytes 8388608
Async XLA Ops:
  0.0 1.0 %copy-start = (bf16[512,512]{1,0:T(8,128)(2,1)S(1)}, bf16[512,512]{1,0:T(8,128)(2,1)}, u32[]{:S(2)}) copy-start(bf16[512,512]{1,0:T(8,128)(2,1)} %keys.1) | copy-start | bytes 1572868
  1.0 1.0 %copy-start.1 = (bf16[512,512]{1,0:T(8,128)(2,1)S(1)}, bf16[512,512]{1,0:T(8,128)(2,1)}, u32[]{:S(2)}) copy-start(bf16[512,512]{1,0:T(8,128)(2,1)} %values.1) | copy-start | bytes 1572868
  2.1 0.7 copy-start.2

commit v2 on v1

--- a/solution.py
+++ b/solution.py
@@ -40,7 +40,7 @@
 
     def weighed(slot, step, top):
         columns = slice(step * TILE, (step + 1) * TILE)
-        weights[slot, :, columns] = jnp.exp2(scores[slot, :, columns] * SCALE - top).astype(
+        weights[slot, :, columns] = jnp.exp2((scores[slot, :, columns] - top) * SCALE).astype(
             jnp.bfloat16
         )
 
@@ -61,11 +61,11 @@
             if pair > 0:
                 weighed(last, step, top)
         if pair < pairs:
-            top = jnp.max(peak, axis=1, keepdims=True) * SCALE
+            top = jnp.max(peak, axis=1, keepdims=True)
         if pair > 0:
             keys_at = pl.ds(pl.multiple_of(first_row, TILE), window)
             total = jnp.dot(weights[last], vx[keys_at, :], preferred_element_type=jnp.float32)
-            result = (total[:, :HEAD_SIZE] / total[:, HEAD_SIZE:]).astype(jnp.bfloat16)
+            result = (total[:, :HEAD_SIZE] * pl.reciprocal(total[:, HEAD_SIZE:])).astype(jnp.bfloat16)
             store(2 * pair - 2, result[:TILE])
             store(2 * pair - 1, result[TILE:])
 
@@ -115,26 +115,28 @@
                 both(lambda kind: copy(mine(head, kind), 0, head, kind, partner).start())
 
     def far(head):
-        both(lambda kind: copy(mine(head, kind), 3, head, kind, ahead).wait_recv())
-
-        @pl.when(odd == 1)
-        def _():
-            both(lambda kind: copy(land.at[3, kind, head], 1, head, kind, across).start())
-
-        @pl.when(core == 1)
-        def _():
-            both(lambda kind: copy(land.at[3, kind, head], 2, head, kind, partner).start())
+        for kind in range(2):
+            copy(mine(head, kind), 3, head, kind, ahead).wait_recv()
+
+            @pl.when(odd == 1)
+            def _():
+                copy(land.at[3, kind, head], 1, head, kind, across).start()
+
+            @pl.when(core == 1)
+            def _():
+                copy(land.at[3, kind, head], 2, head, kind, partner).start()
 
     def near(head):
-        both(lambda kind: copy(mine(head, kind), 1, head, kind, across).wait_recv())
-
-        @pl.when(core == 0)
-        def _():
-            both(lambda kind: copy(land.at[1, kind, head], 2, head, kind, partner).start())
-
-        @pl.when(core == 1)
-        def _():
-            both(lambda kind: copy(land.at[1, kind, head], 0, head, kind, partner).start())
+        for kind in range(2):
+            copy(mine(head, kind), 1, head, kind, across).wait_recv()
+
+            @pl.when(core == 0)
+            def _():
+                copy(land.at[1, kind, head], 2, head, kind, partner).start()
+
+            @pl.when(core == 1)
+            def _():
+                copy(land.at[1, kind, head], 0, head, kind, partner).start()
 
     def beside(head):
         for slot in (0, 2):
@@ -177,19 +179,30 @@
             ).astype(jnp.bfloat16)
         vx[:, HEAD_SIZE:] = jnp.ones((vx.shape[0], HEAD_SIZE), jnp.bfloat16)
 
+    def fill(slot, head):
+        span = slice(reach - (slot + 1) * depth, reach - slot * depth)
+        kt[:HEAD_SIZE, span] = land[slot, 0, head].T
+        vx[span, :HEAD_SIZE] = land[slot, 1, head]
+
     for head in range(groups):
 
         @pl.when((group == head) & (tile == 0))
         def _():
-            if head == 0:
-                far(0)
-                near(0)
-                far(1)
-            beside(head)
             span = slice(reach, reach + depth)
             columns = slice(head * HEAD_SIZE, (head + 1) * HEAD_SIZE)
             kt[:HEAD_SIZE, span] = keys[:, columns].T
             vx[span, :HEAD_SIZE] = values[:, columns]
+            if head == 0:
+                far(0)
+            fill(3, head)
+            if head == 0:
+                near(0)
+            fill(1, head)
+            beside(head)
+            if head == 0:
+                far(1)
+            fill(0, head)
+            fill(2, head)
 
         if head + 1 < groups:
 
@@ -198,13 +211,6 @@
                 near(head + 1)
                 if head + 2 < groups:
                     far(head + 2)
-
-    @pl.when(tile == 0)
-    def _():
-        for slot in range(SPAN_DEV):
-            span = slice(reach - (slot + 1) * depth, reach - slot * depth)
-            kt[:HEAD_SIZE, span] = land[slot, 0, group].T
-            vx[span, :HEAD_SIZE] = land[slot, 1, group]
 
     def query_of(head):
         return q[:, head * HEAD_SIZE : (head + 1) * HEAD_SIZE]
@@ -236,8 +242,8 @@
         out_shape=jax.ShapeDtypeStruct(queries.shape, jnp.bfloat16),
         in_specs=[
             pl.BlockSpec(memory_space=pltpu.SMEM),
-            pl.BlockSpec(memory_space=pltpu.VMEM),
-            pl.BlockSpec(memory_space=pltpu.VMEM),
+            pl.BlockSpec(keys.shape, lambda g, t: (0, 0)),
+            pl.BlockSpec(values.shape, lambda g, t: (0, 0)),
             pl.BlockSpec((TILE, wide), lambda g, t: (t, g)),
         ],
         out_specs=pl.BlockSpec((TILE, wide), lambda g, t: (t, g)),

time: 79.5 us -> 75.4 us (0.948); the launches traced: 78.3 us -> 75.1 us
  Pallas kernels: 73.5 us -> 70.4 us
    pallas_call x1, Pallas kernels: 73.5 us -> 70.4 us  [body(): pl.pallas_call(kernel, grid=(KEY_VALUE_HEADS, row_total // TILE), out_sha...]
where the time goes in v2:
time: 75.4 us; the launch traced here: 75.1 us
  Pallas kernels  70.4 us (93%)
  local copies, waits for them, and re-layouts  4.75 us (6%)
    pallas_call x1, Pallas kernels, body(): pl.pallas_call(kernel, grid=(KEY_VALUE_HEADS, row_total // TILE), out_sha...  70.4 us
    unnamed x7, local copies, waits for them, and re-layouts  4.75 us

profile of v2, /device:TPU:0, one launch (start us, length us, event | category | flops | bytes accessed | tf_op | source)
XLA Modules:
  0.0 75.1 jit_solution(390845030990133716)
XLA Ops:
  0.0 0.0 copy-start
  0.0 1.0 %copy-done = bf16[512,512]{1,0:T(8,128)(2,1)S(1)} copy-done((bf16[512,512]{1,0:T(8,128)(2,1)S(1)}, bf16[512,512]{1,0:T(8,128)(2,1)}, u32[]{:S(2)}) %copy-start) | copy-done | bytes 524312
  1.0 0.0 copy-start.1
  1.0 1.0 %copy-done.1 = bf16[512,512]{1,0:T(8,128)(2,1)S(1)} copy-done((bf16[512,512]{1,0:T(8,128)(2,1)S(1)}, bf16[512,512]{1,0:T(8,128)(2,1)}, u32[]{:S(2)}) %copy-start.1) | copy-done | bytes 524312
  2.1 0.0 copy-start.2
  2.1 0.7 copy-done.2
  2.7 70.4 %shard_map.46 = bf16[512,4096]{1,0:T(8,128)(2,1)S(1)} custom-call(s32[8]{0:T(128)S(1)} %copy-done.2, bf16[512,512]{1,0:T(8,128)(2,1)S(1)} %copy-done, bf16[512,512]{1,0:T(8,128)(2,1)S(1)} %copy-done.1, bf16[512,4096]{1,0:T(8,128)(2,1)} %q.1), custom_call_target="tpu_custom_call" | custom-call | tf_op jit(solution)/shard_map/pallas_call | solution.py:239
  73.1 2.0 %copy.6 = bf16[512,4096]{1,0:T(8,128)(2,1)} copy(bf16[512,4096]{1,0:T(8,128)(2,1)S(1)} %shard_map.46) | data formatting | bytes 8388608
Async XLA Ops:
  0.0 1.0 %copy-start = (bf16[512,512]{1,0:T(8,128)(2,1)S(1)}, bf16[512,512]{1,0:T(8,128)(2,1)}, u32[]{:S(2)}) copy-start(bf16[512,512]{1,0:T(8,128)(2,1)} %keys.1) | copy-start | bytes 1572868
  1.0 1.0 %copy-start.1 = (bf16[512,512]{1,0:T(8,128)(2,1)S(1)}, bf16[512,512]{1,0:T(8,128)(2,1)}, u32[]{:S(2)}) copy-start(bf16[512,512]{1,0:T(8,128)(2,1)} %values.1) | copy-start | bytes 1572868
  2.1 0.7 copy-start.2

commit v3 on v2

--- a/solution.py
+++ b/solution.py
@@ -258,7 +258,7 @@
             pltpu.SemaphoreType.DMA(travel),
         ],
         compiler_params=pltpu.CompilerParams(
-            vmem_limit_bytes=48 * 1024 * 1024, collective_id=0, has_side_effects=True
+            vmem_limit_bytes=67043328, collective_id=0, has_side_effects=True
         ),
     )(doc_lengths, keys, values, queries)
 

time: 75.4 us -> 76.1 us (level)
  Pallas kernels: 70.4 us -> 71.3 us
    pallas_call x1, Pallas kernels: 70.4 us -> 71.3 us  [body(): pl.pallas_call(kernel, grid=(KEY_VALUE_HEADS, row_total // TILE), out_sha...]
    unnamed x7 -> x1, local copies, waits for them, and re-layouts: 4.75 us -> 4.7 us
where the time goes in v3:
time: 76.1 us; the launch traced here: 76 us
  Pallas kernels  71.3 us (94%)
  local copies, waits for them, and re-layouts  4.7 us (6%)
    pallas_call x1, Pallas kernels, body(): pl.pallas_call(kernel, grid=(KEY_VALUE_HEADS, row_total // TILE), out_sha...  71.3 us
    unnamed x1, local copies, waits for them, and re-layouts  4.7 us

profile of v3, /device:TPU:0, one launch (start us, length us, event | category | flops | bytes accessed | tf_op | source)
XLA Modules:
  0.0 76.0 jit_solution(807736252606326863)
XLA Ops:
  0.0 71.3 %shard_map.46 = bf16[512,4096]{1,0:T(8,128)(2,1)} custom-call(s32[8]{0:T(128)} %lengths.1, bf16[512,512]{1,0:T(8,128)(2,1)} %keys.1, bf16[512,512]{1,0:T(8,128)(2,1)} %values.1, bf16[512,4096]{1,0:T(8,128)(2,1)} %q.1), custom_call_target="tpu_custom_call" | custom-call | tf_op jit(solution)/shard_map/pallas_call | solution.py:239
  71.3 4.7 %copy.6 = bf16[512,4096]{1,0:T(8,128)(2,1)} copy(bf16[512,4096]{1,0:T(8,128)(2,1)} %shard_map.46) | data formatting | bytes 8388608
